TPU v7x, 32 devices: a whole 2x2x4 slice. The times are simulated.
32 devices in a mesh: leaf: 8 (over z, y), fsdp: 4 (over x, core).
Axes of the slice: x: 2, y: 2, z: 4, core: 2. Of those that a mesh axis runs over, the one named last changes fastest.
Arguments:
- hidden: bfloat16 [4, 2048, 768], P('fsdp', 'leaf'), may hold values from -6 to 6
- noise_mask: int32 [4, 2048], P('fsdp', 'leaf'), may hold values 0 or 1
- seg_blocks: int32 [4, 128], P('fsdp'), may hold values from 0 to 12, as said below
- parents: int32 [4, 13], P('fsdp'), may hold values from 0 to 4, as said below
- ln1_gain: bfloat16 [768], P(('leaf', 'fsdp')), may hold values from 0.099609375 to 1.8984375
- w_qkv: bfloat16 [768, 2304], P(('leaf', 'fsdp')), may hold values from -0.21875 to 0.21875
- w_out: bfloat16 [768, 768], P(('leaf', 'fsdp')), may hold values from -3.5 to 3.5
- ln2_gain: bfloat16 [768], P(('leaf', 'fsdp')), may hold values from 0.099609375 to 1.8984375
- w_up: bfloat16 [768, 3072], P(('leaf', 'fsdp')), may hold values from -0.21875 to 0.21875
- up_bias: bfloat16 [3072], P(('leaf', 'fsdp')), may hold values from -3 to 3
- w_down: bfloat16 [3072, 768], P(('leaf', 'fsdp')), may hold values from -0.109375 to 0.109375
- down_bias: bfloat16 [768], P(('leaf', 'fsdp')), may hold values from -2 to 2
- mask_embed: bfloat16 [768], P(('leaf', 'fsdp')), may hold values from -5 to 5
- cotangent: bfloat16 [4, 2, 2048, 768], P('fsdp', None, 'leaf'), may hold values from -6 to 6
Outputs:
- output: bfloat16 [4, 2, 2048, 768], P('fsdp', None, 'leaf')
- grad_hidden: bfloat16 [4, 2048, 768], P('fsdp', 'leaf')
- grad_ln1_gain: float32 [768], P(('leaf', 'fsdp'))
- grad_w_qkv: float32 [768, 2304], P(('leaf', 'fsdp'))
- grad_w_out: float32 [768, 768], P(('leaf', 'fsdp'))
- grad_ln2_gain: float32 [768], P(('leaf', 'fsdp'))
- grad_w_up: float32 [768, 3072], P(('leaf', 'fsdp'))
- grad_up_bias: float32 [3072], P(('leaf', 'fsdp'))
- grad_w_down: float32 [3072, 768], P(('leaf', 'fsdp'))
- grad_down_bias: float32 [768], P(('leaf', 'fsdp'))
- grad_mask_embed: float32 [768], P(('leaf', 'fsdp'))
Inputs may be any that keep to these rules, and one draw needn't show every extreme that they name: `seg_blocks`: segment numbers never fall along a tree; segment 0 holds the first 64 blocks (rounded down); every other segment has one block or more; the last segment ends the tree. `parents`: segment 0 is the trunk with parent 0; segments 1 to 4 have parent 0; each of them is the parent of exactly 2 of the segments above 4.
All inputs are finite; a program needn't handle non-finite values. No bound on the sum of `noise_mask` on one device may be relied on, other than what follows from the above.
Results may differ from a plain program's by a relative error of at most 0.015.
Values may be sent and summed in bfloat16 or wider, within the bound.
No kernel may reach another device: no remote copies, remote signals or barrier semaphores. Data moves between devices by JAX's collectives and lax.ppermute only.
A program may use at most 256 MiB of HBM per device.

v0:
```python
import math
import jax
import jax.numpy as jnp
from jax import lax
from jax.sharding import PartitionSpec as P

HEAD_DIM = 64
BLOCK = 16
NEG_FILL = -1000000000.0
EPSILON = 1e-05


def look_up(table, indices):
    slots = jnp.arange(table.shape[0], dtype=jnp.int32)
    hits = indices[..., None] == slots
    return jnp.sum(jnp.where(hits, table, 0), axis=-1)


def tree_layout(seg_row, parent_row):
    slots = jnp.arange(parent_row.shape[0], dtype=jnp.int32)
    seg_lengths = jnp.sum((seg_row[:, None] == slots).astype(jnp.int32), axis=0)
    seg_starts = jnp.cumsum(seg_lengths) - seg_lengths
    grand_parent = look_up(parent_row, parent_row)
    offsets = jnp.where(slots > 0, look_up(seg_lengths, parent_row), 0) + jnp.where(
        parent_row > 0, look_up(seg_lengths, grand_parent), 0
    )
    block_ids = jnp.arange(seg_row.shape[0], dtype=jnp.int32)
    path_block = look_up(offsets, seg_row) + block_ids - look_up(seg_starts, seg_row)
    return (path_block, look_up(parent_row, seg_row), look_up(grand_parent, seg_row))


def layer_norm(values, gain):
    centred = values - jnp.mean(values, axis=-1, keepdims=True)
    spread = jnp.mean(centred * centred, axis=-1, keepdims=True)
    return centred * lax.rsqrt(spread + EPSILON) * gain


def gelu_tanh(values):
    return jax.nn.gelu(values, approximate=True)


def rotate(values, cosine, sine):
    half = values.shape[-1] // 2
    first = values[..., :half]
    second = values[..., half:]
    return jnp.concatenate(
        [first * cosine - second * sine, second * cosine + first * sine], axis=-1
    )


def to_heads(values, heads):
    return values.reshape(values.shape[0], heads, HEAD_DIM).transpose(1, 0, 2)


def from_heads(values):
    return values.transpose(1, 0, 2).reshape(values.shape[1], values.shape[0] * values.shape[2])


def shards(
    hidden,
    noise_mask,
    seg_blocks,
    parents,
    ln1_gain,
    w_qkv,
    w_out,
    ln2_gain,
    w_up,
    up_bias,
    w_down,
    down_bias,
    mask_embed,
    cotangent,
):
    gathered = (
        lax.all_gather(ln1_gain, ("leaf", "fsdp"), axis=0, tiled=True),
        lax.all_gather(w_qkv, ("leaf", "fsdp"), axis=0, tiled=True),
        lax.all_gather(w_out, ("leaf", "fsdp"), axis=0, tiled=True),
        lax.all_gather(ln2_gain, ("leaf", "fsdp"), axis=0, tiled=True),
        lax.all_gather(w_up, ("leaf", "fsdp"), axis=0, tiled=True),
        lax.all_gather(up_bias, ("leaf", "fsdp"), axis=0, tiled=True),
        lax.all_gather(w_down, ("leaf", "fsdp"), axis=0, tiled=True),
        lax.all_gather(down_bias, ("leaf", "fsdp"), axis=0, tiled=True),
        lax.all_gather(mask_embed, ("leaf", "fsdp"), axis=0, tiled=True),
    )
    gain_one, qkv_w, out_w, gain_two, up_w, up_b, down_w, down_b, embed = gathered
    rows_dev = hidden.shape[1]
    width = hidden.shape[2]
    heads = width // HEAD_DIM
    blocks_dev = rows_dev // BLOCK
    leaf_rank = lax.axis_index("leaf")
    seg_row = seg_blocks[0]
    path_block, first_up, second_up = tree_layout(seg_row, parents[0])
    first_block = leaf_rank * blocks_dev
    own_seg = lax.dynamic_slice_in_dim(seg_row, first_block, blocks_dev)
    own_path = lax.dynamic_slice_in_dim(path_block, first_block, blocks_dev)
    own_first = lax.dynamic_slice_in_dim(first_up, first_block, blocks_dev)
    own_second = lax.dynamic_slice_in_dim(second_up, first_block, blocks_dev)
    related = (
        (seg_row[None, :] == own_seg[:, None])
        | (seg_row[None, :] == own_first[:, None])
        | (seg_row[None, :] == own_second[:, None])
    )
    clean_ok = related & (path_block[None, :] <= own_path[:, None])
    noisy_ok = related & (path_block[None, :] < own_path[:, None])
    clean_tok = jnp.repeat(jnp.repeat(clean_ok, BLOCK, axis=0), BLOCK, axis=1)
    noisy_tok = jnp.repeat(jnp.repeat(noisy_ok, BLOCK, axis=0), BLOCK, axis=1)
    row_block = jnp.arange(rows_dev, dtype=jnp.int32) // BLOCK
    same_block = row_block[:, None] == row_block[None, :]
    mask_all = jnp.concatenate(
        [
            jnp.concatenate([clean_tok, jnp.zeros_like(same_block)], axis=1),
            jnp.concatenate([noisy_tok, same_block], axis=1),
        ],
        axis=0,
    )
    offsets_in = jnp.arange(BLOCK, dtype=jnp.int32)
    positions = (own_path[:, None] * BLOCK + offsets_in).reshape(rows_dev).astype(jnp.float32)
    positions = jnp.concatenate([positions, positions])
    freqs = jnp.exp(
        jnp.arange(HEAD_DIM // 2, dtype=jnp.float32) * (-math.log(10000.0) / (HEAD_DIM // 2))
    )
    angles = positions[:, None, None] * freqs
    cosine = jnp.cos(angles)
    sine = jnp.sin(angles)
    clean = hidden[0].astype(jnp.float32)
    masked = (noise_mask[0] == 1)[:, None]
    noisy = jnp.where(masked, embed.astype(jnp.float32)[None, :], clean)
    stream = jnp.concatenate([clean, noisy], axis=0)
    gain_one_f = gain_one.astype(jnp.float32)
    gain_two_f = gain_two.astype(jnp.float32)
    normed_one = layer_norm(stream, gain_one_f).astype(jnp.bfloat16)
    projected = jnp.dot(normed_one, qkv_w, preferred_element_type=jnp.float32)
    query = rotate(
        projected[:, :width].reshape(2 * rows_dev, heads, HEAD_DIM), cosine, sine
    ).reshape(2 * rows_dev, width)
    keyed = rotate(
        projected[:, width : 2 * width].reshape(2 * rows_dev, heads, HEAD_DIM), cosine, sine
    ).reshape(2 * rows_dev, width)
    query_low = query.astype(jnp.bfloat16)
    key_low = keyed.astype(jnp.bfloat16)
    value_low = projected[:, 2 * width :].astype(jnp.bfloat16)
    tree_keys, tree_values = (
        lax.all_gather(key_low[:rows_dev], "leaf", axis=0, tiled=True),
        lax.all_gather(value_low[:rows_dev], "leaf", axis=0, tiled=True),
    )
    tree_tok = tree_keys.shape[0]
    keys_all = jnp.concatenate([tree_keys, key_low[rows_dev:]], axis=0)
    values_all = jnp.concatenate([tree_values, value_low[rows_dev:]], axis=0)
    q_heads = to_heads(query_low, heads)

    def head_forward(operands):
        q_head, k_head, v_head = operands
        raw = jnp.einsum("qd,kd->qk", q_head, k_head, preferred_element_type=jnp.float32) * 0.125
        scores = jnp.where(mask_all, raw, NEG_FILL)
        top_score = jnp.max(scores, axis=-1, keepdims=True)
        expd = jnp.exp(scores - top_score)
        total = jnp.sum(expd, axis=-1, keepdims=True)
        probs = (expd / total).astype(jnp.bfloat16)
        return (
            jnp.dot(probs, v_head, preferred_element_type=jnp.float32),
            top_score + jnp.log(total),
        )

    attended, log_norm = lax.map(
        head_forward, (q_heads, to_heads(keys_all, heads), to_heads(values_all, heads))
    )
    mixed_low = from_heads(attended).astype(jnp.bfloat16)
    after = stream + jnp.dot(mixed_low, out_w, preferred_element_type=jnp.float32)
    normed_two = layer_norm(after, gain_two_f).astype(jnp.bfloat16)
    pre_act = jnp.dot(normed_two, up_w, preferred_element_type=jnp.float32) + up_b.astype(
        jnp.float32
    )
    activated = gelu_tanh(pre_act).astype(jnp.bfloat16)
    result = (
        after
        + jnp.dot(activated, down_w, preferred_element_type=jnp.float32)
        + down_b.astype(jnp.float32)
    )
    output = result.astype(jnp.bfloat16).reshape(1, 2, rows_dev, width)
    regathered = (
        lax.all_gather(ln1_gain, ("leaf", "fsdp"), axis=0, tiled=True),
        lax.all_gather(w_qkv, ("leaf", "fsdp"), axis=0, tiled=True),
        lax.all_gather(w_out, ("leaf", "fsdp"), axis=0, tiled=True),
        lax.all_gather(ln2_gain, ("leaf", "fsdp"), axis=0, tiled=True),
        lax.all_gather(w_up, ("leaf", "fsdp"), axis=0, tiled=True),
        lax.all_gather(up_bias, ("leaf", "fsdp"), axis=0, tiled=True),
        lax.all_gather(w_down, ("leaf", "fsdp"), axis=0, tiled=True),
        lax.all_gather(down_bias, ("leaf", "fsdp"), axis=0, tiled=True),
        lax.all_gather(mask_embed, ("leaf", "fsdp"), axis=0, tiled=True),
    )
    qkv_back, out_back, up_back, down_back = (
        regathered[1],
        regathered[2],
        regathered[4],
        regathered[6],
    )
    grad_out = cotangent[0].astype(jnp.float32).reshape(2 * rows_dev, width)
    grad_two = grad_out.astype(jnp.bfloat16)
    grad_down_b = jnp.sum(grad_two.astype(jnp.float32), axis=0)
    grad_down_w = jnp.einsum("rf,rd->fd", activated, grad_two, preferred_element_type=jnp.float32)
    grad_act = jnp.einsum("rd,fd->rf", grad_two, down_back, preferred_element_type=jnp.float32)
    gelu_out, gelu_back = jax.vjp(gelu_tanh, pre_act)
    grad_pre = gelu_back(grad_act)[0].astype(jnp.bfloat16)
    grad_up_b = jnp.sum(grad_pre.astype(jnp.float32), axis=0)
    grad_up_w = jnp.einsum("rd,rf->df", normed_two, grad_pre, preferred_element_type=jnp.float32)
    grad_normed_two = jnp.einsum("rf,df->rd", grad_pre, up_back, preferred_element_type=jnp.float32)
    norm_out, norm_back = jax.vjp(layer_norm, after, gain_two_f)
    grad_after_ln, grad_gain_two = norm_back(grad_normed_two)
    grad_after = grad_out + grad_after_ln
    grad_one = grad_after.astype(jnp.bfloat16)
    grad_out_w = jnp.einsum("rd,re->de", mixed_low, grad_one, preferred_element_type=jnp.float32)
    grad_mixed = jnp.einsum(
        "re,de->rd", grad_one, out_back, preferred_element_type=jnp.float32
    ).astype(jnp.bfloat16)
    back_keys, back_values = (
        lax.all_gather(key_low[:rows_dev], "leaf", axis=0, tiled=True),
        lax.all_gather(value_low[:rows_dev], "leaf", axis=0, tiled=True),
    )
    keys_back = jnp.concatenate([back_keys, key_low[rows_dev:]], axis=0)
    values_back = jnp.concatenate([back_values, value_low[rows_dev:]], axis=0)

    def head_backward(operands):
        q_head, k_head, v_head, g_head, norm_head = operands
        raw = jnp.einsum("qd,kd->qk", q_head, k_head, preferred_element_type=jnp.float32) * 0.125
        scores = jnp.where(mask_all, raw, NEG_FILL)
        probs = jnp.exp(scores - norm_head)
        grad_v = jnp.einsum(
            "qk,qd->kd", probs.astype(jnp.bfloat16), g_head, preferred_element_type=jnp.float32
        )
        grad_p = jnp.einsum("qd,kd->qk", g_head, v_head, preferred_element_type=jnp.float32)
        inner = jnp.sum(probs * grad_p, axis=-1, keepdims=True)
        grad_s = (probs * (grad_p - inner)).astype(jnp.bfloat16)
        grad_q = jnp.einsum("qk,kd->qd", grad_s, k_head, preferred_element_type=jnp.float32) * 0.125
        grad_k = jnp.einsum("qk,qd->kd", grad_s, q_head, preferred_element_type=jnp.float32) * 0.125
        return (grad_q, grad_k, grad_v)

    grad_q_heads, grad_k_heads, grad_v_heads = lax.map(
        head_backward,
        (
            q_heads,
            to_heads(keys_back, heads),
            to_heads(values_back, heads),
            to_heads(grad_mixed, heads),
            log_norm,
        ),
    )
    grad_query = from_heads(grad_q_heads)
    grad_keys_all = from_heads(grad_k_heads)
    grad_values_all = from_heads(grad_v_heads)
    own_key_grad, own_value_grad = (
        lax.psum_scatter(
            grad_keys_all[:tree_tok].astype(jnp.bfloat16), "leaf", scatter_dimension=0, tiled=True
        ).astype(jnp.float32),
        lax.psum_scatter(
            grad_values_all[:tree_tok].astype(jnp.bfloat16), "leaf", scatter_dimension=0, tiled=True
        ).astype(jnp.float32),
    )
    grad_key = jnp.concatenate([own_key_grad, grad_keys_all[tree_tok:]], axis=0)
    grad_value = jnp.concatenate([own_value_grad, grad_values_all[tree_tok:]], axis=0)
    grad_query = rotate(grad_query.reshape(2 * rows_dev, heads, HEAD_DIM), cosine, -sine).reshape(
        2 * rows_dev, width
    )
    grad_key = rotate(grad_key.reshape(2 * rows_dev, heads, HEAD_DIM), cosine, -sine).reshape(
        2 * rows_dev, width
    )
    grad_proj = jnp.concatenate([grad_query, grad_key, grad_value], axis=1).astype(jnp.bfloat16)
    grad_qkv_w = jnp.einsum("rd,re->de", normed_one, grad_proj, preferred_element_type=jnp.float32)
    grad_normed_one = jnp.einsum(
        "re,de->rd", grad_proj, qkv_back, preferred_element_type=jnp.float32
    )
    first_out, first_back = jax.vjp(layer_norm, stream, gain_one_f)
    grad_stream_ln, grad_gain_one = first_back(grad_normed_one)
    grad_stream = grad_after + grad_stream_ln
    grad_clean = grad_stream[:rows_dev] + jnp.where(masked, 0.0, grad_stream[rows_dev:])
    grad_embed = jnp.sum(jnp.where(masked, grad_stream[rows_dev:], 0.0), axis=0)
    summed = (
        lax.psum_scatter(grad_gain_one, ("leaf", "fsdp"), scatter_dimension=0, tiled=True),
        lax.psum_scatter(grad_qkv_w, ("leaf", "fsdp"), scatter_dimension=0, tiled=True),
        lax.psum_scatter(grad_out_w, ("leaf", "fsdp"), scatter_dimension=0, tiled=True),
        lax.psum_scatter(grad_gain_two, ("leaf", "fsdp"), scatter_dimension=0, tiled=True),
        lax.psum_scatter(grad_up_w, ("leaf", "fsdp"), scatter_dimension=0, tiled=True),
        lax.psum_scatter(grad_up_b, ("leaf", "fsdp"), scatter_dimension=0, tiled=True),
        lax.psum_scatter(grad_down_w, ("leaf", "fsdp"), scatter_dimension=0, tiled=True),
        lax.psum_scatter(grad_down_b, ("leaf", "fsdp"), scatter_dimension=0, tiled=True),
        lax.psum_scatter(grad_embed, ("leaf", "fsdp"), scatter_dimension=0, tiled=True),
    )
    return (
        output,
        grad_clean.astype(jnp.bfloat16)[None],
        summed[0],
        summed[1],
        summed[2],
        summed[3],
        summed[4],
        summed[5],
        summed[6],
        summed[7],
        summed[8],
    )


def solution(mesh):
    in_specs = (
        P("fsdp", "leaf", None),
        P("fsdp", "leaf"),
        P("fsdp", None),
        P("fsdp", None),
        P(("leaf", "fsdp")),
        P(("leaf", "fsdp"), None),
        P(("leaf", "fsdp"), None),
        P(("leaf", "fsdp")),
        P(("leaf", "fsdp"), None),
        P(("leaf", "fsdp")),
        P(("leaf", "fsdp"), None),
        P(("leaf", "fsdp")),
        P(("leaf", "fsdp")),
        P("fsdp", None, "leaf", None),
    )
    out_specs = (
        P("fsdp", None, "leaf", None),
        P("fsdp", "leaf", None),
        P(("leaf", "fsdp")),
        P(("leaf", "fsdp"), None),
        P(("leaf", "fsdp"), None),
        P(("leaf", "fsdp")),
        P(("leaf", "fsdp"), None),
        P(("leaf", "fsdp")),
        P(("leaf", "fsdp"), None),
        P(("leaf", "fsdp")),
        P(("leaf", "fsdp")),
    )
    return jax.shard_map(shards, mesh=mesh, in_specs=in_specs, out_specs=out_specs, check_vma=False)
```

profile of v0, /device:TPU:0, one launch (start us, length us, event | category | flops | bytes accessed | tf_op | source)
XLA Modules:
  0.0 1240.7 jit_solution(11994550310879820292)
XLA Ops:
  12.2 42.3 %all-reduce.12 = (bf16[768]{0:T(1024)(128)(2,1)S(1)}, bf16[768]{0:T(1024)(128)(2,1)S(1)}, bf16[768]{0:T(1024)(128)(2,1)}, bf16[768]{0:T(1024)(128)(2,1)S(1)}, bf16[3072]{0:T(1024)(128)(2,1)S(1)}) all-reduce(bf16[768]{0:T(1024)(128)(2,1)S(1)} %dynamic-update-slice.1, ...), channel_id=1, replica_groups=mesh['leaf'=8,'fsdp'=4] {'leaf','fsdp'}, use_global_device_ids=true, to_apply=%add.2 | all-reduce | flops 6144 | bytes 24576
  58.5 15.2 %all-gather.7.cloned.1.call-done = bf16[768,2304]{1,0:T(8,128)(2,1)} async-done(((bf16[24,2304]{1,0:T(8,128)(2,1)}), bf16[768,2304]{1,0:T(8,128)(2,1)}) %all-gather.7.cloned.1.call-update) | async-done | bytes 3538960 | tf_op jit(solution)/shard_map/all_gather | solution.py:77
  73.8 6.2 fusion.73
  83.0 3.9 fusion.71
  88.9 3.0 copy.76
  91.9 2.7 subtract_convert_fusion.2
  105.6 34.7 %all-gather.11.cloned.1.call-done = bf16[2048,768]{1,0:T(8,128)(2,1)} async-done(((bf16[256,768]{1,0:T(8,128)(2,1)}), bf16[2048,768]{1,0:T(8,128)(2,1)}) %all-gather.11.cloned.1.call-update) | async-done | bytes 3145744 | tf_op jit(solution)/shard_map/all_gather | solution.py:145
  140.3 4.0 pad_maximum_fusion.1
  144.3 5.9 copy.80
  150.2 53.8 %all-gather.9.cloned.1.call-done = bf16[2048,768]{0,1:T(8,128)(2,1)} async-done(((bf16[256,768]{0,1:T(8,128)(2,1)}), bf16[2048,768]{0,1:T(8,128)(2,1)}) %all-gather.9.cloned.1.call-update) | async-done | bytes 3145744 | tf_op jit(solution)/shard_map/all_gather | solution.py:144
  204.1 4.0 pad_maximum_fusion
  208.1 7.9 copy.82
  216.0 8.0 copy.84
  224.0 69.5 %while.28 = (s32[]{:T(128)}, bf16[12,512,64]{1,2,0:T(8,128)(2,1)S(1)}, f32[12,512,1]{1,2,0:T(1,128)}, bf16[12,512,64]{2,1,0:T(8,128)(2,1)}, bf16[12,2304,64]{2,1...) while((s32[]{:T(128)}, ...), condition=%wide.region_14.15_spmd.clone, body=%wide.region_11.14_spmd.sunk.clone | while | flops 311426560 | bytes 16799832 | solution.py:165
  297.5 27.0 %all-gather.15.cloned.1.call-done = bf16[768,3072]{1,0:T(8,128)(2,1)} async-done(((bf16[24,3072]{1,0:T(8,128)(2,1)}), bf16[768,3072]{1,0:T(8,128)(2,1)}) %all-gather.15.cloned.1.call-update) | async-done | bytes 4718608 | tf_op jit(solution)/shard_map/all_gather | solution.py:80
  324.5 8.2 fusion.64
  332.7 57.0 %all-gather.17.cloned.1.call-done = bf16[3072,768]{1,0:T(8,128)(2,1)} async-done(((bf16[96,768]{1,0:T(8,128)(2,1)}), bf16[3072,768]{1,0:T(8,128)(2,1)}) %all-gather.17.cloned.1.call-update) | async-done | bytes 4718608 | tf_op jit(solution)/shard_map/all_gather | solution.py:82
  389.7 9.9 convert_reduce_fusion
  399.6 3.4 multiply_reduce_fusion.1
  410.1 154.7 %while.29 = (s32[]{:T(128)}, f32[12,512,64]{1,2,0:T(8,128)}, f32[12,2304,64]{1,2,0:T(8,128)}, bf16[12,2304,64]{1,2,0:T(8,128)(2,1)}, bf16[12,512,64]{2,1,0:T(8,1...) while((s32[]{:T(128)}, f32[12,512,64]{1,2,0:T(8,128)}, ...), condition=%wide.region_21.22_spmd.clone, body=%wide.region_19.21_spmd.sunk.clone | while | flops 765771264 | bytes 40057968 | solution.py:238
  412.7 2.8 multiply_reduce_fusion.9
  425.5 2.8 multiply_reduce_fusion.9
  438.4 2.8 multiply_reduce_fusion.9
  451.3 2.8 multiply_reduce_fusion.9
  464.2 2.8 multiply_reduce_fusion.9
  469.6 2.6 fusion.139
  477.0 2.8 multiply_reduce_fusion.9
  489.9 2.8 multiply_reduce_fusion.9
  502.8 2.8 multiply_reduce_fusion.9
  515.7 2.8 multiply_reduce_fusion.9
  528.6 2.8 multiply_reduce_fusion.9
  541.5 2.8 multiply_reduce_fusion.9
  554.4 2.8 multiply_reduce_fusion.9
  559.8 2.6 fusion.139
  564.7 4.9 slice.169
  569.7 3.9 slice.123
  574.8 3.5 fusion.75
  578.3 10.1 fusion.66
  589.9 7.2 fusion.63
  601.2 42.4 %reduce-scatter.7.cloned.1.call-done = bf16[256,768]{0,1:T(8,128)(2,1)} async-done(((bf16[2048,768]{0,1:T(8,128)(2,1)}), bf16[256,768]{0,1:T(8,128)(2,1)}) %reduce-scatter.7.cloned.1.call-update) | async-done | bytes 393232 | tf_op jit(solution)/shard_map/reduce_scatter | solution.py:252
  648.9 72.4 %reduce-scatter.9.cloned.1.call-done = bf16[256,768]{0,1:T(8,128)(2,1)} async-done(((bf16[2048,768]{0,1:T(8,128)(2,1)}), bf16[256,768]{0,1:T(8,128)(2,1)}) %reduce-scatter.9.cloned.1.call-update) | async-done | bytes 393232 | tf_op jit(solution)/shard_map/reduce_scatter | solution.py:255
  721.3 6.7 fusion.52
  730.6 9.3 add_convert_fusion
  745.6 40.2 %all-reduce.11 = (f32[768]{0:T(1024)S(1)}, f32[768]{0:T(1024)S(1)}, f32[3072]{0:T(1024)S(1)}, f32[768]{0:T(1024)S(1)}, f32[768]{0:T(1024)S(1)}) all-reduce(f32[768]{0:T(1024)S(1)} %get-tuple-element.195, f32[768]{0:T(1024)S(1)} %copy-done.34, f32[3072]{0:T(1024)S(1)} %copy-done.31, ...), channel_id=4, replica_groups=mesh['leaf'=8,'fsdp'=4] {'leaf','fsdp'}, use_global_device_ids=true, to_apply=%region_27.28.clone | all-reduce | flops 6144 | bytes 49152
  788.8 36.7 %reduce-scatter.13.cloned.1.call-done = f32[24,768]{1,0:T(8,128)} async-done(((f32[768,768]{1,0:T(8,128)}), f32[24,768]{1,0:T(8,128)}) %reduce-scatter.13.cloned.1.call-update) | async-done | bytes 73744 | tf_op jit(solution)/shard_map/reduce_scatter | solution.py:280
  825.5 141.8 %reduce-scatter.17.cloned.1.call-done = f32[96,768]{1,0:T(8,128)} async-done(((f32[3072,768]{1,0:T(8,128)}), f32[96,768]{1,0:T(8,128)}) %reduce-scatter.17.cloned.1.call-update) | async-done | bytes 294928 | tf_op jit(solution)/shard_map/reduce_scatter | solution.py:284
  967.3 141.1 %reduce-scatter.15.cloned.1.call-done = f32[24,3072]{1,0:T(8,128)} async-done(((f32[768,3072]{1,0:T(8,128)}), f32[24,3072]{1,0:T(8,128)}) %reduce-scatter.15.cloned.1.call-update) | async-done | bytes 294928 | tf_op jit(solution)/shard_map/reduce_scatter | solution.py:282
  1108.4 125.2 %reduce-scatter.11.cloned.1.call-done = f32[24,2304]{1,0:T(8,128)} async-done(((f32[768,2304]{1,0:T(8,128)}), f32[24,2304]{1,0:T(8,128)}) %reduce-scatter.11.cloned.1.call-update) | async-done | bytes 221200 | tf_op jit(solution)/shard_map/reduce_scatter | solution.py:279
  (324 shorter events, 243.5 us)
Async XLA Ops:
  7.2 66.6 %all-gather.7.cloned.1.call-start = ((), (), s32[]{:S(2)}) async-start(), calls=%async_computation.6 | async-start | bytes 3649536 | tf_op jit(solution)/shard_map/all_gather | solution.py:77
  7.9 132.4 %all-gather.11.cloned.1.call-start = ((), (), s32[]{:S(2)}) async-start(), calls=%async_computation.8 | async-start | bytes 3538944 | tf_op jit(solution)/shard_map/all_gather | solution.py:145
  54.5 19.2 %copy-start.26 = (f32[768]{0:T(1024)}, f32[768]{0:T(1024)S(1)}, u32[]{:S(2)}) copy-start(f32[768]{0:T(1024)S(1)} %convert_element_type.105) | copy-start | bytes 9220
  55.2 2.7 copy-start.35
  57.6 22.4 %copy-start.22 = (f32[512]{0:T(512)}, f32[512]{0:T(512)S(1)}, u32[]{:S(2)}) copy-start(f32[512]{0:T(512)S(1)} %broadcast_multiply_fusion.1) | copy-start | bytes 6148
  58.5 21.5 %copy-start.24 = (f32[512]{0:T(512)}, f32[512]{0:T(512)S(1)}, u32[]{:S(2)}) copy-start(f32[512]{0:T(512)S(1)} %fusion.57) | copy-start | bytes 6148
  58.5 22.5 %copy-start.37 = (s32[1,128]{1,0:T(1,128)S(1)}, s32[1,128]{1,0:T(1,128)}, u32[]{:S(2)}) copy-start(s32[1,128]{1,0:T(1,128)} %param.20) | copy-start | bytes 1540
  58.5 22.8 %copy-start.33 = (s32[1,13]{1,0:T(1,128)S(1)}, s32[1,13]{1,0:T(1,128)}, u32[]{:S(2)}) copy-start(s32[1,13]{1,0:T(1,128)} %param.21) | copy-start | bytes 160
  81.0 123.1 %all-gather.9.cloned.1.call-start = ((), (), s32[]{:S(2)}) async-start(), calls=%async_computation.7 | async-start | bytes 3538944 | tf_op jit(solution)/shard_map/all_gather | solution.py:144
  83.0 8.9 copy-start.18
  95.6 197.8 %all-gather.13.cloned.1.call-start = ((), (), s32[]{:S(2)}) async-start(), calls=%async_computation.9 | async-start | bytes 1216512 | tf_op jit(solution)/shard_map/all_gather | solution.py:78
  96.2 228.2 %all-gather.15.cloned.1.call-start = ((), (), s32[]{:S(2)}) async-start(), calls=%async_computation.10 | async-start | bytes 4866048 | tf_op jit(solution)/shard_map/all_gather | solution.py:80
  96.8 292.9 %all-gather.17.cloned.1.call-start = ((), (), s32[]{:S(2)}) async-start(), calls=%async_computation.11 | async-start | bytes 4866048 | tf_op jit(solution)/shard_map/all_gather | solution.py:82
  97.4 546.2 %reduce-scatter.7.cloned.1.call-start = ((), (), s32[]{:S(2)}) async-start(), calls=%async_computation.12 | async-start | bytes 3538944 | tf_op jit(solution)/shard_map/reduce_scatter | solution.py:252
  100.4 3.5 copy-start.14
  100.5 3.5 copy-start.15
  144.3 59.8 %copy-start.13 = (bf16[256,12,64]{0,2,1:T(8,128)(2,1)S(1)}, bf16[256,12,64]{0,2,1:T(8,128)(2,1)}, u32[]{:S(2)}) copy-start(bf16[256,12,64]{0,2,1:T(8,128)(2,1)} %get-tuple-element.274) | copy-start | bytes 1179652
  216.0 8.0 copy-start.8
  293.4 2.5 copy-start.9
  295.9 1.2 copy-start.2
  297.4 92.3 %copy-start.5 = (bf16[1,2,256,768]{3,2,1,0:T(8,128)(2,1)S(1)}, bf16[1,2,256,768]{3,2,1,0:T(8,128)(2,1)}, u32[]{:S(2)}) copy-start(bf16[1,2,256,768]{3,2,1,0:T(8,128)(2,1)} %param.31) | copy-start | bytes 2359300
  389.7 9.9 copy-start.3
  389.7 9.9 copy-start.38
  399.6 3.4 copy-start.12
  403.7 2.3 copy-start.39
  569.7 151.7 %reduce-scatter.9.cloned.1.call-start = ((), (), s32[]{:S(2)}) async-start(), calls=%async_computation.13 | async-start | bytes 3538944 | tf_op jit(solution)/shard_map/reduce_scatter | solution.py:255
  573.7 4.6 copy-start.32
  573.7 251.8 %reduce-scatter.13.cloned.1.call-start = ((), (), s32[]{:S(2)}) async-start(), calls=%async_computation.15 | async-start | bytes 2433024 | tf_op jit(solution)/shard_map/reduce_scatter | solution.py:280
  578.3 389.1 %reduce-scatter.17.cloned.1.call-start = ((), (), s32[]{:S(2)}) async-start(), calls=%async_computation.17 | async-start | bytes 9732096 | tf_op jit(solution)/shard_map/reduce_scatter | solution.py:284
  588.4 1.4 copy-start.4
  588.5 520.0 %reduce-scatter.15.cloned.1.call-start = ((), (), s32[]{:S(2)}) async-start(), calls=%async_computation.16 | async-start | bytes 9732096 | tf_op jit(solution)/shard_map/reduce_scatter | solution.py:282
  597.0 47.6 %copy-start.19 = (f32[512,32]{0,1:T(8,128)S(1)}, f32[512,32]{0,1:T(8,128)}, u32[]{:S(2)}) copy-start(f32[512,32]{0,1:T(8,128)} %copy-done.18) | copy-start | bytes 196612
  597.1 47.6 %copy-start.21 = (f32[512,32]{0,1:T(8,128)S(1)}, f32[512,32]{0,1:T(8,128)}, u32[]{:S(2)}) copy-start(f32[512,32]{0,1:T(8,128)} %get-tuple-element.281) | copy-start | bytes 196612
  597.1 636.5 %reduce-scatter.11.cloned.1.call-start = ((), (), s32[]{:S(2)}) async-start(), calls=%async_computation.14 | async-start | bytes 7299072 | tf_op jit(solution)/shard_map/reduce_scatter | solution.py:279
  646.9 74.4 %copy-start.20 = (bf16[256,12,64]{0,2,1:T(8,128)(2,1)S(1)}, bf16[256,12,64]{0,2,1:T(8,128)(2,1)}, u32[]{:S(2)}) copy-start(bf16[256,12,64]{0,2,1:T(8,128)(2,1)} %slice.124) | copy-start | bytes 1179652
  646.9 74.4 %copy-start.23 = (f32[512]{0:T(512)S(1)}, f32[512]{0:T(512)}, u32[]{:S(2)}) copy-start(f32[512]{0:T(512)} %copy-done.22) | copy-start | bytes 6148
  647.0 74.4 %copy-start.25 = (f32[512]{0:T(512)S(1)}, f32[512]{0:T(512)}, u32[]{:S(2)}) copy-start(f32[512]{0:T(512)} %copy-done.24) | copy-start | bytes 6148
  647.0 74.4 %copy-start.27 = (f32[768]{0:T(1024)S(1)}, f32[768]{0:T(1024)}, u32[]{:S(2)}) copy-start(f32[768]{0:T(1024)} %copy-done.26) | copy-start | bytes 9220
  730.6 9.3 copy-start.7
  730.6 9.3 copy-start.16
  730.6 9.3 copy-start.17
  730.6 9.3 copy-start.40
  739.9 2.5 copy-start.29
  742.4 1.4 copy-start.1
  742.4 1.6 copy-start.6
  744.0 1.6 copy-start.30
  744.0 1.6 copy-start.31
  744.0 1.6 copy-start.34
  (5 other events, 4.4 us)
Sparse Core Ops, SparseCore 0:
  10.9 62.7 all-gather.6
  81.1 59.1 all-gather.10
  142.3 61.6 all-gather.8
  206.8 52.2 all-gather.12
  261.9 62.5 all-gather.14
  327.2 62.4 all-gather.16
  569.8 73.7 reduce-scatter.6
  647.2 74.0 reduce-scatter.8
  727.2 98.2 reduce-scatter.12
  832.8 134.4 reduce-scatter.16
  973.8 134.5 reduce-scatter.14
  1115.5 118.0 reduce-scatter.10
where the time goes:
time: 1250 us; the launch traced here: 1240 us
  waiting for transfers between devices  750 us (60%)
  matrix products  264 us (21%)
  blocking collectives  82.6 us (7%)
  local copies, waits for them, and re-layouts  80.2 us (6%)
  other arithmetic  47 us (4%)
  between operations  15 us (1%)
    reduce_scatter x1, waiting for transfers between devices, shards(): lax.psum_scatter(grad_down_w, ('leaf', 'fsdp'), scatter_dimension=0, tile...  142 us
    reduce_scatter x1, waiting for transfers between devices, shards(): lax.psum_scatter(grad_up_w, ('leaf', 'fsdp'), scatter_dimension=0, tiled=...  141 us
    reduce_scatter x1, waiting for transfers between devices, shards(): lax.psum_scatter(grad_qkv_w, ('leaf', 'fsdp'), scatter_dimension=0, tiled...  125 us
    unnamed x2, blocking collectives  82.6 us
    reduce_scatter x1, waiting for transfers between devices, shards(): lax.psum_scatter(grad_values_all[:tree_tok].astype(jnp.bfloat16), 'leaf',...  72.4 us
    all_gather x1, waiting for transfers between devices, shards(): lax.all_gather(w_down, ('leaf', 'fsdp'), axis=0, tiled=True)  57 us
    all_gather x1, waiting for transfers between devices, shards(): lax.all_gather(key_low[:rows_dev], 'leaf', axis=0, tiled=True)  53.8 us
    reduce_scatter x1, waiting for transfers between devices, shards(): lax.psum_scatter(grad_keys_all[:tree_tok].astype(jnp.bfloat16), 'leaf', s...  42.4 us
  transfers between devices with their start and end apart: 12, of which 11 were waited for; matrix products, arithmetic and copies ran while one was open for 16% of the time, Pallas kernels for 0%

commit v1 on v0

--- a/solution.py
+++ b/solution.py
@@ -3,11 +3,29 @@
 import jax.numpy as jnp
 from jax import lax
 from jax.sharding import PartitionSpec as P
+from jax.lax import axis_index, axis_size, ppermute
 
 HEAD_DIM = 64
 BLOCK = 16
 NEG_FILL = -1000000000.0
 EPSILON = 1e-05
+
+
+def marks_extend(payload, axis_name):
+    long_array, response, part_now = (axis_size(axis_name), axis_index(axis_name), payload.shape[0])
+    h_now, y1 = (payload, 1)
+    while y1 < long_array:
+        h_now = jnp.concatenate(
+            [
+                h_now,
+                ppermute(
+                    h_now, axis_name, tuple(((s, (s - y1) % long_array) for s in range(long_array)))
+                ),
+            ],
+            0,
+        )
+        y1 = 2 * y1
+    return jnp.roll(h_now, response * part_now, 0)
 
 
 def look_up(table, indices):
@@ -141,7 +159,7 @@
     key_low = keyed.astype(jnp.bfloat16)
     value_low = projected[:, 2 * width :].astype(jnp.bfloat16)
     tree_keys, tree_values = (
-        lax.all_gather(key_low[:rows_dev], "leaf", axis=0, tiled=True),
+        marks_extend(key_low[:rows_dev], "leaf"),
         lax.all_gather(value_low[:rows_dev], "leaf", axis=0, tiled=True),
     )
     tree_tok = tree_keys.shape[0]

time: 1250 us -> 1310 us (1.048)
  waiting for transfers between devices: 750 us -> 796 us
    ppermute x0 -> x3, waiting for transfers between devices: none -> 146 us  [marks_extend(): ppermute(h_now, axis_name, tuple(((s, (s - y1) % long_array) for s in ran...]
    all_gather x1, waiting for transfers between devices: 53.8 us -> 0.01 us  [shards(): lax.all_gather(key_low[:rows_dev], 'leaf', axis=0, tiled=True)]
    all_gather x1, waiting for transfers between devices: 34.7 us -> 0.01 us  [shards(): lax.all_gather(value_low[:rows_dev], 'leaf', axis=0, tiled=True)]
  transfers between devices with their start and end apart: 12 -> 15, of which waited for: 11 -> 12; matrix products, arithmetic and copies ran while one was open for 16% -> 16% of each run, Pallas kernels for 0% -> 0%
where the time goes in v1:
time: 1310 us; the launch traced here: 1300 us
  waiting for transfers between devices  796 us (61%)
  matrix products  260 us (20%)
  blocking collectives  82.6 us (6%)
  local copies, waits for them, and re-layouts  80 us (6%)
  other arithmetic  56.2 us (4%)
  between operations  15.1 us (1%)
    ppermute x3, waiting for transfers between devices, marks_extend(): ppermute(h_now, axis_name, tuple(((s, (s - y1) % long_array) for s in ran...  146 us
    reduce_scatter x1, waiting for transfers between devices, shards(): lax.psum_scatter(grad_down_w, ('leaf', 'fsdp'), scatter_dimension=0, tile...  142 us
    reduce_scatter x1, waiting for transfers between devices, shards(): lax.psum_scatter(grad_up_w, ('leaf', 'fsdp'), scatter_dimension=0, tiled=...  141 us
    reduce_scatter x1, waiting for transfers between devices, shards(): lax.psum_scatter(grad_qkv_w, ('leaf', 'fsdp'), scatter_dimension=0, tiled...  125 us
    unnamed x2, blocking collectives  82.6 us
    reduce_scatter x1, waiting for transfers between devices, shards(): lax.psum_scatter(grad_values_all[:tree_tok].astype(jnp.bfloat16), 'leaf',...  72.5 us
    all_gather x1, waiting for transfers between devices, shards(): lax.all_gather(w_down, ('leaf', 'fsdp'), axis=0, tiled=True)  57 us
    reduce_scatter x1, waiting for transfers between devices, shards(): lax.psum_scatter(grad_keys_all[:tree_tok].astype(jnp.bfloat16), 'leaf', s...  42.4 us
  transfers between devices with their start and end apart: 15, of which 12 were waited for; matrix products, arithmetic and copies ran while one was open for 16% of the time, Pallas kernels for 0%

profile of v1, /device:TPU:0, one launch (start us, length us, event | category | flops | bytes accessed | tf_op | source)
XLA Modules:
  0.0 1297.7 jit_solution(11792042012681535285)
XLA Ops:
  12.2 42.3 %all-reduce.12 = (bf16[768]{0:T(1024)(128)(2,1)S(1)}, bf16[768]{0:T(1024)(128)(2,1)S(1)}, bf16[768]{0:T(1024)(128)(2,1)}, bf16[768]{0:T(1024)(128)(2,1)}, bf16[3072]{0:T(1024)(128)(2,1)S(1)}) all-reduce(bf16[768]{0:T(1024)(128)(2,1)S(1)} %dynamic-update-slice.1, ...), channel_id=1, replica_groups=mesh['leaf'=8,'fsdp'=4] {'leaf','fsdp'}, use_global_device_ids=true, to_apply=%add.2 | all-reduce | flops 6144 | bytes 24576
  58.5 15.2 %all-gather.7.cloned.1.call-done = bf16[768,2304]{1,0:T(8,128)(2,1)} async-done(((bf16[24,2304]{1,0:T(8,128)(2,1)}), bf16[768,2304]{1,0:T(8,128)(2,1)}) %all-gather.7.cloned.1.call-update) | async-done | bytes 3538960 | tf_op jit(solution)/shard_map/all_gather | solution.py:95
  73.7 6.2 fusion.73
  84.0 3.8 fusion.71
  89.8 3.0 copy.76
  92.8 2.7 subtract_convert_fusion.2
  97.8 3.2 collective-permute-start
  100.9 9.4 collective-permute-done
  111.4 3.1 collective-permute-start.1
  117.3 38.8 %collective-permute-done.1 = bf16[512,768]{0,1:T(8,128)(2,1)S(1)} collective-permute-done((bf16[512,768]{0,1:T(8,128)(2,1)S(1)}, bf16[512,768]{0,1:T(8,128)(2,1)S(1)}, u32[]{:S(2)}, u32[]{:S(2)}) %collective-permute-start.1) | collective-permute-done | bytes 786464 | tf_op jit(solution)/shard_map/ppermute | solution.py:21
  170.6 97.3 %collective-permute-done.2 = bf16[1024,768]{0,1:T(8,128)(2,1)} collective-permute-done((bf16[1024,768]{0,1:T(8,128)(2,1)}, bf16[1024,768]{0,1:T(8,128)(2,1)}, u32[]{:S(2)}, u32[]{:S(2)}) %collective-permute-start.2) | collective-permute-done | bytes 1572896 | tf_op jit(solution)/shard_map/ppermute | solution.py:21
  273.3 3.9 pad_maximum_fusion.2
  277.3 5.8 copy.80
  283.1 7.9 copy.84
  291.0 5.2 pad_maximum_fusion
  296.2 67.9 %while.28 = (s32[]{:T(128)}, bf16[12,512,64]{1,2,0:T(8,128)(2,1)S(1)}, f32[12,512,1]{1,2,0:T(1,128)}, bf16[12,512,64]{2,1,0:T(8,128)(2,1)}, bf16[12,2304,64]{1,2...) while((s32[]{:T(128)}, ...), condition=%wide.region_14.15_spmd.clone, body=%wide.region_11.14_spmd.sunk.clone | while | flops 311426560 | bytes 16504921 | solution.py:183
  364.1 2.7 fusion.74
  368.3 16.6 %all-gather.13.cloned.1.call-done = bf16[768,3072]{1,0:T(8,128)(2,1)} async-done(((bf16[24,3072]{1,0:T(8,128)(2,1)}), bf16[768,3072]{1,0:T(8,128)(2,1)}) %all-gather.13.cloned.1.call-update) | async-done | bytes 4718608 | tf_op jit(solution)/shard_map/all_gather | solution.py:98
  384.9 8.2 fusion.64
  393.1 57.0 %all-gather.15.cloned.1.call-done = bf16[3072,768]{1,0:T(8,128)(2,1)} async-done(((bf16[96,768]{1,0:T(8,128)(2,1)}), bf16[3072,768]{1,0:T(8,128)(2,1)}) %all-gather.15.cloned.1.call-update) | async-done | bytes 4718608 | tf_op jit(solution)/shard_map/all_gather | solution.py:100
  450.1 9.9 convert_reduce_fusion
  460.0 3.4 multiply_reduce_fusion.1
  470.5 151.6 %while.29 = (s32[]{:T(128)}, f32[12,512,64]{1,2,0:T(8,128)}, f32[12,2304,64]{1,2,0:T(8,128)}, bf16[12,2304,64]{1,2,0:T(8,128)(2,1)}, bf16[12,512,64]{2,1,0:T(8,1...) while((s32[]{:T(128)}, f32[12,512,64]{1,2,0:T(8,128)}, ...), condition=%wide.region_21.22_spmd.clone, body=%wide.region_19.21_spmd.sunk.clone | while | flops 765771264 | bytes 39468144 | solution.py:256
  485.7 2.7 multiply_reduce_fusion.9
  498.3 2.7 multiply_reduce_fusion.9
  511.0 2.7 multiply_reduce_fusion.9
  523.6 2.7 multiply_reduce_fusion.9
  536.2 2.7 multiply_reduce_fusion.9
  548.9 2.7 multiply_reduce_fusion.9
  561.5 2.7 multiply_reduce_fusion.9
  574.1 2.7 multiply_reduce_fusion.9
  586.7 2.7 multiply_reduce_fusion.9
  599.4 2.7 multiply_reduce_fusion.9
  612.0 2.7 multiply_reduce_fusion.9
  622.1 4.9 slice.169
  627.1 3.9 slice.123
  632.1 3.4 fusion.75
  635.6 10.0 fusion.66
  647.1 7.2 fusion.63
  658.4 42.4 %reduce-scatter.7.cloned.1.call-done = bf16[256,768]{0,1:T(8,128)(2,1)} async-done(((bf16[2048,768]{0,1:T(8,128)(2,1)}), bf16[256,768]{0,1:T(8,128)(2,1)}) %reduce-scatter.7.cloned.1.call-update) | async-done | bytes 393232 | tf_op jit(solution)/shard_map/reduce_scatter | solution.py:270
  706.1 72.5 %reduce-scatter.9.cloned.1.call-done = bf16[256,768]{0,1:T(8,128)(2,1)} async-done(((bf16[2048,768]{0,1:T(8,128)(2,1)}), bf16[256,768]{0,1:T(8,128)(2,1)}) %reduce-scatter.9.cloned.1.call-update) | async-done | bytes 393232 | tf_op jit(solution)/shard_map/reduce_scatter | solution.py:273
  778.5 6.7 fusion.52
  787.8 9.3 add_convert_fusion
  802.6 40.2 %all-reduce.11 = (f32[768]{0:T(1024)S(1)}, f32[768]{0:T(1024)S(1)}, f32[3072]{0:T(1024)S(1)}, f32[768]{0:T(1024)S(1)}, f32[768]{0:T(1024)S(1)}) all-reduce(f32[768]{0:T(1024)S(1)} %get-tuple-element.195, f32[768]{0:T(1024)S(1)} %copy-done.35, f32[3072]{0:T(1024)S(1)} %copy-done.32, ...), channel_id=4, replica_groups=mesh['leaf'=8,'fsdp'=4] {'leaf','fsdp'}, use_global_device_ids=true, to_apply=%region_27.28.clone | all-reduce | flops 6144 | bytes 49152
  845.7 36.8 %reduce-scatter.13.cloned.1.call-done = f32[24,768]{1,0:T(8,128)} async-done(((f32[768,768]{1,0:T(8,128)}), f32[24,768]{1,0:T(8,128)}) %reduce-scatter.13.cloned.1.call-update) | async-done | bytes 73744 | tf_op jit(solution)/shard_map/reduce_scatter | solution.py:298
  882.6 141.7 %reduce-scatter.17.cloned.1.call-done = f32[96,768]{1,0:T(8,128)} async-done(((f32[3072,768]{1,0:T(8,128)}), f32[96,768]{1,0:T(8,128)}) %reduce-scatter.17.cloned.1.call-update) | async-done | bytes 294928 | tf_op jit(solution)/shard_map/reduce_scatter | solution.py:302
  1024.3 141.3 %reduce-scatter.15.cloned.1.call-done = f32[24,3072]{1,0:T(8,128)} async-done(((f32[768,3072]{1,0:T(8,128)}), f32[24,3072]{1,0:T(8,128)}) %reduce-scatter.15.cloned.1.call-update) | async-done | bytes 294928 | tf_op jit(solution)/shard_map/reduce_scatter | solution.py:300
  1165.6 125.1 %reduce-scatter.11.cloned.1.call-done = f32[24,2304]{1,0:T(8,128)} async-done(((f32[768,2304]{1,0:T(8,128)}), f32[24,2304]{1,0:T(8,128)}) %reduce-scatter.11.cloned.1.call-update) | async-done | bytes 221200 | tf_op jit(solution)/shard_map/reduce_scatter | solution.py:297
  (344 shorter events, 261.4 us)
Async XLA Ops:
  7.2 66.6 %all-gather.7.cloned.1.call-start = ((), (), s32[]{:S(2)}) async-start(), calls=%async_computation.6 | async-start | bytes 3649536 | tf_op jit(solution)/shard_map/all_gather | solution.py:95
  7.9 265.4 %all-gather.9.cloned.1.call-start = ((), (), s32[]{:S(2)}) async-start(), calls=%async_computation.7 | async-start | bytes 3538944 | tf_op jit(solution)/shard_map/all_gather | solution.py:163
  54.5 25.4 %copy-start.27 = (f32[768]{0:T(1024)}, f32[768]{0:T(1024)S(1)}, u32[]{:S(2)}) copy-start(f32[768]{0:T(1024)S(1)} %convert_element_type.105) | copy-start | bytes 9220
  55.2 2.7 copy-start.36
  57.6 22.4 %copy-start.23 = (f32[512]{0:T(512)}, f32[512]{0:T(512)S(1)}, u32[]{:S(2)}) copy-start(f32[512]{0:T(512)S(1)} %broadcast_multiply_fusion.1) | copy-start | bytes 6148
  58.5 21.5 %copy-start.25 = (f32[512]{0:T(512)}, f32[512]{0:T(512)S(1)}, u32[]{:S(2)}) copy-start(f32[512]{0:T(512)S(1)} %fusion.57) | copy-start | bytes 6148
  58.5 22.5 %copy-start.38 = (s32[1,128]{1,0:T(1,128)S(1)}, s32[1,128]{1,0:T(1,128)}, u32[]{:S(2)}) copy-start(s32[1,128]{1,0:T(1,128)} %param.20) | copy-start | bytes 1540
  58.5 22.8 %copy-start.34 = (s32[1,13]{1,0:T(1,128)S(1)}, s32[1,13]{1,0:T(1,128)}, u32[]{:S(2)}) copy-start(s32[1,13]{1,0:T(1,128)} %param.21) | copy-start | bytes 160
  80.9 210.0 %all-gather.17.cloned.1.call-start = ((), (), s32[]{:S(2)}) async-start(), calls=%async_computation.11 | async-start | bytes 3538944 | tf_op jit(solution)/shard_map/all_gather | solution.py:235
  84.0 8.8 copy-start.19
  96.5 267.5 %all-gather.11.cloned.1.call-start = ((), (), s32[]{:S(2)}) async-start(), calls=%async_computation.8 | async-start | bytes 1216512 | tf_op jit(solution)/shard_map/all_gather | solution.py:96
  97.1 287.8 %all-gather.13.cloned.1.call-start = ((), (), s32[]{:S(2)}) async-start(), calls=%async_computation.9 | async-start | bytes 4866048 | tf_op jit(solution)/shard_map/all_gather | solution.py:98
  97.7 352.4 %all-gather.15.cloned.1.call-start = ((), (), s32[]{:S(2)}) async-start(), calls=%async_computation.10 | async-start | bytes 4866048 | tf_op jit(solution)/shard_map/all_gather | solution.py:100
  97.8 12.6 collective-permute-start
  111.4 44.7 %collective-permute-start.1 = (bf16[512,768]{0,1:T(8,128)(2,1)S(1)}, bf16[512,768]{0,1:T(8,128)(2,1)S(1)}, u32[]{:S(2)}, u32[]{:S(2)}) collective-permute-start(bf16[512,768]{0,1:T(8,128)(2,1)S(1)} %pad_maximum_fusion.6), channel_id=1, source_target_pairs={{0,24},{4,28},{8,0},{12,4},{16,8},{20,12},{24,16},{28,20},{1,25},{... | collective-permute-start | bytes 2359304 | tf_op jit(solution)/shard_map/ppermute | solution.py:21
  114.5 586.2 %reduce-scatter.7.cloned.1.call-start = ((), (), s32[]{:S(2)}) async-start(), calls=%async_computation.12 | async-start | bytes 3538944 | tf_op jit(solution)/shard_map/reduce_scatter | solution.py:270
  156.1 4.1 copy-start.8
  158.7 109.2 %collective-permute-start.2 = (bf16[1024,768]{0,1:T(8,128)(2,1)}, bf16[1024,768]{0,1:T(8,128)(2,1)}, u32[]{:S(2)}, u32[]{:S(2)}) collective-permute-start(bf16[1024,768]{0,1:T(8,128)(2,1)} %pad_maximum_fusion.4), channel_id=1, source_target_pairs={{0,16},{4,20},{8,24},{12,28},{16,0},{20,4},{24,8},{28,12},{1,17},{... | collective-permute-start | bytes 4718600 | tf_op jit(solution)/shard_map/ppermute | solution.py:21
  162.4 6.8 copy-start
  169.3 100.3 %copy-start.9 = (bf16[512,768]{0,1:T(8,128)(2,1)S(1)}, bf16[512,768]{0,1:T(8,128)(2,1)}, u32[]{:S(2)}) copy-start(bf16[512,768]{0,1:T(8,128)(2,1)} %copy-done.8) | copy-start | bytes 2359300
  271.3 2.0 copy-start.16
  290.9 5.2 copy-start.11
  364.1 4.2 copy-start.12
  368.2 81.8 %copy-start.6 = (bf16[1,2,256,768]{3,2,1,0:T(8,128)(2,1)S(1)}, bf16[1,2,256,768]{3,2,1,0:T(8,128)(2,1)}, u32[]{:S(2)}) copy-start(bf16[1,2,256,768]{3,2,1,0:T(8,128)(2,1)} %param.31) | copy-start | bytes 2359300
  450.1 9.9 copy-start.4
  450.1 9.9 copy-start.40
  460.0 3.4 copy-start.15
  463.4 3.1 copy-start.41
  627.0 151.5 %reduce-scatter.9.cloned.1.call-start = ((), (), s32[]{:S(2)}) async-start(), calls=%async_computation.13 | async-start | bytes 3538944 | tf_op jit(solution)/shard_map/reduce_scatter | solution.py:273
  631.0 4.6 copy-start.33
  631.0 251.5 %reduce-scatter.13.cloned.1.call-start = ((), (), s32[]{:S(2)}) async-start(), calls=%async_computation.15 | async-start | bytes 2433024 | tf_op jit(solution)/shard_map/reduce_scatter | solution.py:298
  635.6 388.7 %reduce-scatter.17.cloned.1.call-start = ((), (), s32[]{:S(2)}) async-start(), calls=%async_computation.17 | async-start | bytes 9732096 | tf_op jit(solution)/shard_map/reduce_scatter | solution.py:302
  645.7 1.4 copy-start.5
  645.7 519.9 %reduce-scatter.15.cloned.1.call-start = ((), (), s32[]{:S(2)}) async-start(), calls=%async_computation.16 | async-start | bytes 9732096 | tf_op jit(solution)/shard_map/reduce_scatter | solution.py:300
  654.3 47.6 %copy-start.20 = (f32[512,32]{0,1:T(8,128)S(1)}, f32[512,32]{0,1:T(8,128)}, u32[]{:S(2)}) copy-start(f32[512,32]{0,1:T(8,128)} %copy-done.19) | copy-start | bytes 196612
  654.3 47.6 %copy-start.22 = (f32[512,32]{0,1:T(8,128)S(1)}, f32[512,32]{0,1:T(8,128)}, u32[]{:S(2)}) copy-start(f32[512,32]{0,1:T(8,128)} %get-tuple-element.283) | copy-start | bytes 196612
  654.3 636.3 %reduce-scatter.11.cloned.1.call-start = ((), (), s32[]{:S(2)}) async-start(), calls=%async_computation.14 | async-start | bytes 7299072 | tf_op jit(solution)/shard_map/reduce_scatter | solution.py:297
  701.9 76.6 %copy-start.24 = (f32[512]{0:T(512)S(1)}, f32[512]{0:T(512)}, u32[]{:S(2)}) copy-start(f32[512]{0:T(512)} %copy-done.23) | copy-start | bytes 6148
  701.9 76.6 %copy-start.26 = (f32[512]{0:T(512)S(1)}, f32[512]{0:T(512)}, u32[]{:S(2)}) copy-start(f32[512]{0:T(512)} %copy-done.25) | copy-start | bytes 6148
  701.9 76.6 %copy-start.28 = (f32[768]{0:T(1024)S(1)}, f32[768]{0:T(1024)}, u32[]{:S(2)}) copy-start(f32[768]{0:T(1024)} %copy-done.27) | copy-start | bytes 9220
  704.2 74.4 %copy-start.21 = (bf16[256,12,64]{0,2,1:T(8,128)(2,1)S(1)}, bf16[256,12,64]{0,2,1:T(8,128)(2,1)}, u32[]{:S(2)}) copy-start(bf16[256,12,64]{0,2,1:T(8,128)(2,1)} %slice.124) | copy-start | bytes 1179652
  787.8 9.3 copy-start.10
  787.8 9.3 copy-start.17
  787.8 9.3 copy-start.18
  787.8 9.3 copy-start.42
  797.1 2.5 copy-start.30
  799.6 1.4 copy-start.2
  799.6 1.6 copy-start.7
  (10 other events, 10.9 us)
Sparse Core Ops, SparseCore 0:
  10.9 62.7 all-gather.6
  81.1 75.0 all-gather.8
  158.2 105.3 all-gather.16
  266.4 52.9 all-gather.10
  322.1 62.7 all-gather.12
  387.6 62.3 all-gather.14
  627.1 73.5 reduce-scatter.6
  704.4 74.0 reduce-scatter.8
  784.4 98.1 reduce-scatter.12
  889.9 134.3 reduce-scatter.16
  1030.8 134.7 reduce-scatter.14
  1172.6 117.9 reduce-scatter.10
